TPU v7x, 32 devices: a whole 2x2x4 slice. The times are simulated.
32 devices in a mesh: dp: 4 (over y, x), tp: 8 (over z, core).
Axes of the slice: x: 2, y: 2, z: 4, core: 2. Of those that a mesh axis runs over, the one named last changes fastest.
Arguments:
- hidden_in: bfloat16 [4, 32, 4096], P(None, 'dp'), may hold values from -6 to 6
- pre_gain: float32 [4096], replicated, may hold values from 0.25 to 1.75
- w_zx: bfloat16 [4096, 2, 8192], P(None, None, 'tp'), may hold values from -0.09375 to 0.09375
- zx_codes: bfloat16 [4096, 2, 8192], P(('dp', 'tp')), may hold values from -4 to 4
- zx_exponents: int32 [32, 2, 64], P('dp', None, 'tp'), may hold values from -9 to -6
- w_bc: bfloat16 [4096, 2048], P(None, 'tp'), may hold values from -0.09375 to 0.09375
- w_dt: bfloat16 [4096, 128], P(None, 'tp'), may hold values from -0.09375 to 0.09375
- conv_x: float32 [5, 8192], P(None, 'tp'), may hold values from -0.6 to 0.6
- conv_bc: float32 [5, 2048], P(None, 'tp'), may hold values from -0.6 to 0.6
- dt_bias: float32 [128], P('tp'), may hold values from -2 to 0.5
- decay_rate: float32 [128], P('tp'), may hold values from 0.05 to 2
- skip_gain: float32 [128], P('tp'), may hold values from 0.5 to 1.5
- conv_state_x: bfloat16 [32, 3, 8192], P('dp', None, 'tp'), may hold values from -6 to 6
- conv_state_bc: bfloat16 [32, 3, 2048], P('dp', None, 'tp'), may hold values from -6 to 6
- ssm_state: float32 [32, 128, 64, 256], P('dp', 'tp'), may hold values from -6 to 6
- norm_gain: float32 [8192], P('tp'), may hold values from 0.25 to 1.75
- w_out: bfloat16 [8192, 4096], P('tp'), may hold values from -0.0625 to 0.0625
- out_codes: bfloat16 [8192, 4096], P('tp', 'dp'), may hold values from -4 to 4
- out_exponents: int32 [64, 32], P('tp', 'dp'), may hold values from -7 to -4
Outputs:
- mixed: bfloat16 [4, 32, 4096], P(None, 'dp', 'tp')
- final_state: float32 [32, 128, 64, 256], P('dp', 'tp')
All inputs are finite; a program needn't handle non-finite values.
Results may differ from a plain program's by a relative error of at most 0.014.
Values may be sent and summed in bfloat16 or wider, within the bound.
A program may use at most 192 MiB of HBM per device.

v0:
```python
import jax
import jax.numpy as jnp
from jax import lax
from jax.sharding import PartitionSpec as P

D = 4096
H = 128
G = 4
BLK = 128
STEPS = 4
DI = 8192
EPS = 1e-05


def decode_pairs(codes, exponents, block):
    rows, pair, cols = codes.shape
    blocked = codes.astype(jnp.float32).reshape(rows // block, block, pair, cols // block, block)
    scales = jnp.exp2(exponents.astype(jnp.float32))
    return (blocked * scales[:, None, :, :, None]).reshape(rows, pair, cols)


def decode_matrix(codes, exponents, block):
    rows, cols = codes.shape
    blocked = codes.astype(jnp.float32).reshape(rows // block, block, cols // block, block)
    scales = jnp.exp2(exponents.astype(jnp.float32))
    return (blocked * scales[:, None, :, None]).reshape(rows, cols)


def conv_step(history, fresh, params):
    window = jnp.concatenate([history, fresh[:, None, :]], axis=1)
    mixed = jnp.sum(window * params[:4][None], axis=1) + params[4]
    return (jax.nn.silu(mixed), window[:, 1:])


def body(
    hidden_in,
    pre_gain,
    w_zx,
    zx_codes,
    zx_exponents,
    w_bc,
    w_dt,
    conv_x,
    conv_bc,
    dt_bias,
    decay_rate,
    skip_gain,
    conv_state_x,
    conv_state_bc,
    ssm_state,
    norm_gain,
    w_out,
    out_codes,
    out_exponents,
):
    slot = lax.axis_index("tp")
    tp_count = lax.axis_size("tp")
    traded = lax.all_to_all(zx_codes, "tp", split_axis=2, concat_axis=0, tiled=True)
    zx_delta = decode_pairs(traded, zx_exponents, BLK)
    local_cols = traded.shape[2]
    gathered = lax.all_gather(zx_delta.astype(jnp.bfloat16), "dp", axis=0, tiled=True)
    zx_weights = (
        (w_zx.astype(jnp.float32) + gathered.astype(jnp.float32))
        .astype(jnp.bfloat16)
        .reshape(D, 2 * local_cols)
    )
    out_piece = decode_matrix(out_codes, out_exponents, BLK).astype(jnp.bfloat16)
    out_full = lax.all_gather(out_piece, "dp", axis=1, tiled=True)
    new_out = (w_out.astype(jnp.float32) + out_full.astype(jnp.float32)).astype(jnp.bfloat16)
    heads_here = ssm_state.shape[1]
    states_n = ssm_state.shape[3]
    group = slot * heads_here // (H // G)
    group_mask = (jnp.arange(G) == group).astype(jnp.float32)
    history_x = conv_state_x.astype(jnp.float32)
    history_bc = conv_state_bc.astype(jnp.float32)
    state = ssm_state
    results = []
    carried = None
    for step in range(STEPS):
        x = hidden_in[step].astype(jnp.float32)
        if step > 0:
            x = x + carried.astype(jnp.float32)
        rows = x.shape[0]
        normed = (x * lax.rsqrt(jnp.mean(x * x, -1, keepdims=True) + EPS) * pre_gain).astype(
            jnp.bfloat16
        )
        zx = jnp.dot(normed, zx_weights, preferred_element_type=jnp.float32)
        zx = zx.reshape(rows, 2, local_cols)
        gate = zx[:, 0]
        inner = zx[:, 1]
        bc_raw = jnp.dot(normed, w_bc, preferred_element_type=jnp.float32)
        dt_raw = jnp.dot(normed, w_dt, preferred_element_type=jnp.float32)
        conv_inner, history_x = conv_step(history_x, inner, conv_x)
        conv_piece, history_bc = conv_step(history_bc, bc_raw, conv_bc)
        bc_all = lax.all_gather(conv_piece, "tp", axis=1, tiled=True)
        b_group = lax.dynamic_slice_in_dim(bc_all, group * states_n, states_n, 1)
        c_group = lax.dynamic_slice_in_dim(bc_all, G * states_n + group * states_n, states_n, 1)
        step_size = jax.nn.softplus(dt_raw + dt_bias)
        decay = jnp.exp(-step_size * decay_rate)
        inner_heads = conv_inner.reshape(rows, heads_here, -1)
        state = (
            decay[:, :, None, None] * state
            + (step_size[:, :, None] * inner_heads)[:, :, :, None] * b_group[:, None, None, :]
        )
        read = (
            jnp.einsum("rhpn,rn->rhp", state, c_group, precision=lax.Precision.HIGHEST)
            + skip_gain[:, None] * inner_heads
        )
        gated = read.reshape(rows, local_cols) * jax.nn.silu(gate)
        squares = jnp.sum(gated * gated, -1)
        totals = lax.psum(squares[:, None] * group_mask, "tp")
        mean_sq = jnp.sum(totals * group_mask, -1) / (DI // G)
        scaled = (gated * lax.rsqrt(mean_sq + EPS)[:, None] * norm_gain).astype(jnp.bfloat16)
        partial_value = jnp.dot(scaled, new_out, preferred_element_type=jnp.float32)
        whole = lax.psum(partial_value, "tp").astype(jnp.bfloat16)
        width = partial_value.shape[1] // tp_count
        results.append(lax.dynamic_slice_in_dim(whole, slot * width, width, 1))
        carried = whole
    return (jnp.stack(results), state)


def solution(mesh):
    return jax.shard_map(
        body,
        mesh=mesh,
        in_specs=(
            P(None, "dp", None),
            P(),
            P(None, None, "tp"),
            P(("dp", "tp"), None, None),
            P("dp", None, "tp"),
            P(None, "tp"),
            P(None, "tp"),
            P(None, "tp"),
            P(None, "tp"),
            P("tp"),
            P("tp"),
            P("tp"),
            P("dp", None, "tp"),
            P("dp", None, "tp"),
            P("dp", "tp", None, None),
            P("tp"),
            P("tp", None),
            P("tp", "dp"),
            P("tp", "dp"),
        ),
        out_specs=(P(None, "dp", "tp"), P("dp", "tp", None, None)),
        check_vma=False,
    )
```

profile of v0, /device:TPU:0, one launch (start us, length us, event | category | flops | bytes accessed | tf_op | source)
XLA Modules:
  0.0 712.7 jit_solution(7525767807919478908)
XLA Ops:
  7.2 0.8 multiply_exponential_fusion.4
  8.1 0.3 mul.639
  8.4 4.1 fusion.3
  12.6 15.0 %copy.29 = bf16[128,2,8192]{0,1,2:T(2,128)(2,1)} copy(bf16[128,2,8192]{2,1,0:T(2,128)(2,1)} %param.22) | data formatting | bytes 8388608 | tf_op args[3]
  27.6 6.4 all-to-all-start
  34.1 4.0 mul.609
  38.1 10.8 %mul.610 = f32[1024,2,1024]{2,1,0:T(2,128)} reshape(f32[8,128,2,8,128]{4,3,2,1,0:T(8,128)} %mul.609) | data formatting | bytes 16777216 | tf_op jit(solution)/shard_map/mul | solution.py:19
  48.8 79.2 %all-to-all-done = bf16[128,2,8192]{0,1,2:T(2,128)(2,1)} async-done(((bf16[128,2,8192]{0,1,2:T(2,128)(2,1)}), bf16[128,2,8192]{0,1,2:T(2,128)(2,1)}, u32[]{:S(2)}, u32[]{:S(2)}) %all-to-all-start) | async-done | bytes 4194336 | tf_op jit(solution)/shard_map/all_to_all | solution.py:58
  128.1 8.5 %convert_bitcast_fusion = f32[8,128,2,1024]{1,2,3,0:T(2,128)} fusion(bf16[128,2,8,1024]{0,1,3,2:T(2,128)(2,1)} %bitcast.39), kind=kLoop, calls=%fused_computation.2 | loop fusion | flops 2097152 | bytes 12582912 | tf_op jit(solution)/shard_map/convert_element_type | solution.py:17
  136.5 17.1 %copy.30 = f32[8,128,2,1024]{3,2,1,0:T(2,128)} copy(f32[8,128,2,1024]{1,2,3,0:T(2,128)} %convert_bitcast_fusion) | data formatting | bytes 16777216 | tf_op jit(solution)/shard_map/convert_element_type | solution.py:17
  153.7 9.0 %fusion = bf16[1024,2,1024]{2,1,0:T(2,128)(2,1)} fusion(f32[1024,2,1024]{2,1,0:T(2,128)} %mul.610, f32[8,128,2,1024]{3,2,1,0:T(2,128)} %copy.30), kind=kLoop, calls=%fused_computation.4 | loop fusion | flops 4194304 | bytes 20971520 | tf_op jit(solution)/shard_map/convert_element_type | solution.py:61
  163.2 0.4 convolution_bitcast_fusion.3
  163.6 14.2 %all_gather.19 = f32[8,2048]{1,0:T(8,128)S(1)} all-gather(f32[8,256]{1,0:T(8,128)S(1)} %divide_multiply_fusion.7), channel_id=1, replica_groups=mesh['dp'=4,'tp'=8] {'tp'}, dimensions={1}, use_global_device_ids=true | all-gather | bytes 73728 | tf_op jit(solution)/shard_map/all_gather | solution.py:95
  178.1 10.1 %add_convert_fusion.1 = bf16[1024,4096]{1,0:T(8,128)(2,1)} fusion(bf16[1024,4096]{1,0:T(8,128)(2,1)} %all-gather.5.cloned.1.call-done, bf16[1024,4096]{1,0:T(8,128)(2,1)} %param.35), kind=kLoop, calls=%fused_computation.1 | loop fusion | flops 16777216 | bytes 25165824 | tf_op jit(solution)/shard_map/convert_element_type | solution.py:69
  188.2 131.0 %all-gather.3.cloned.1.call-done = bf16[4096,2,1024]{2,1,0:T(2,128)(2,1)} async-done(((bf16[1024,2,1024]{2,1,0:T(2,128)(2,1)}), bf16[4096,2,1024]{2,1,0:T(2,128)(2,1)}) %all-gather.3.cloned.1.call-update) | async-done | bytes 16777232 | tf_op jit(solution)/shard_map/all_gather | solution.py:61
  319.1 19.2 %add_convert_fusion = bf16[4096,2,1024]{2,1,0:T(2,128)(2,1)S(1)} fusion(bf16[4096,2,1024]{2,1,0:T(2,128)(2,1)} %all-gather.3.cloned.1.call-done, bf16[4096,2,1024]{2,1,0:T(2,128)(2,1)} %param.21), kind=kLoop, calls=%fused_computation | loop fusion | flops 33554432 | bytes 50331648 | tf_op jit(solution)/shard_map/convert_element_type | solution.py:64
  338.3 9.3 %copy.40 = bf16[512,8,2,1024]{3,1,2,0:T(8,128)(2,1)} copy(bf16[512,8,2,1024]{3,2,1,0:T(2,128)(2,1)S(1)} %bitcast.210) | data formatting | bytes 33554432
  347.6 20.7 %copy.31 = bf16[2048,4096]{1,0:T(8,128)(2,1)} copy(bf16[2048,4096]{0,1:T(8,128)(2,1)} %bitcast.211) | data formatting | bytes 33554432 | tf_op jit(solution)/shard_map/dot_general | solution.py:87
  368.3 10.2 %fusion.29 = f32[8,2,1024]{2,0,1:T(8,128)S(1)} fusion(bf16[2,1024,4096]{2,1,0:T(8,128)(2,1)} %bitcast.206, f32[4096]{0:T(1024)S(1)} %copy-done.5, f32[8]{0:T(128)S(1)} %add_rsqrt_fusion.7, bf16[4,8,4096]{2,1,0:T(8,128)(2,1)S(1)} %copy-done.2), kind=kOutput, calls=%fused_computation.67 | convolution fusion | flops 134348800 | bytes 16925184 | tf_op jit(solution)/shard_map/dot_general | solution.py:87
  378.8 13.1 %fusion.1 = f32[8,1,16,64]{3,1,2,0:T(1,128)S(1)} fusion(f32[8,16,64,256]{3,2,1,0:T(8,128)} %param.33, f32[8,256]{1,0:T(8,128)S(1)} %get-tuple-element.23, f32[8,16,64]{2,1,0:T(8,128)S(1)} %broadcast_multiply_fusion.3, f32[8,16]{1,0:T(8,128)S(1)} %get-tuple-element.26, f32[8,256,1,1]{1,0,2,3:T(8,128)S(1)} %get-tuple-element.22), kind=kOutput, calls=%fused_computation.9 | convolution fusion | flops 31457280 | bytes 8471040 | tf_op jit(solution)/shard_map/rhpn,rn->rhp/dot_general | solution.py:106
  391.9 0.2 multiply_reduce_fusion.6
  392.2 16.4 %psum.56 = f32[8,4]{0,1:T(4,128)S(1)} all-reduce(f32[8,4]{0,1:T(4,128)S(1)} %broadcast_multiply_fusion.7), channel_id=1, replica_groups=mesh['dp'=4,'tp'=8] {'tp'}, use_global_device_ids=true, to_apply=%region_4.5 | all-reduce | flops 32 | bytes 256 | tf_op jit(solution)/shard_map/psum | solution.py:111
  408.8 4.6 fusion.84
  413.4 27.1 %all-reduce.4 = bf16[8,4096]{1,0:T(8,128)(2,1)S(1)} all-reduce(f32[8,4096]{1,0:T(8,128)S(1)} %fusion.84), channel_id=1, replica_groups=mesh['dp'=4,'tp'=8] {'tp'}, use_global_device_ids=true, to_apply=%region_6.7 | all-reduce | flops 32768 | bytes 196608 | tf_op jit(solution)/shard_map/psum | solution.py:115
  440.8 10.2 %fusion.35 = f32[8,2,1024]{2,0,1:T(8,128)S(1)} fusion(bf16[2,1024,4096]{2,1,0:T(8,128)(2,1)} %bitcast.207, bf16[8,4096]{1,0:T(8,128)(2,1)S(1)} %multiply_convert_fusion.2), kind=kOutput, calls=%fused_computation.72 | convolution fusion | flops 134217728 | bytes 16908288 | tf_op jit(solution)/shard_map/dot_general | solution.py:87
  451.2 0.4 convolution_bitcast_fusion.2
  451.7 14.0 %all_gather.21 = f32[8,2048]{1,0:T(8,128)S(1)} all-gather(f32[8,256]{1,0:T(8,128)S(1)} %divide_multiply_fusion.6), channel_id=1, replica_groups=mesh['dp'=4,'tp'=8] {'tp'}, dimensions={1}, use_global_device_ids=true | all-gather | bytes 73728 | tf_op jit(solution)/shard_map/all_gather | solution.py:95
  465.9 13.7 %fusion.10 = f32[8,1,16,64]{3,1,2,0:T(1,128)S(1)} fusion(f32[8,16,64,256]{3,2,1,0:T(8,128)} %param.33, f32[8,256]{1,0:T(8,128)S(1)} %get-tuple-element.19, f32[8,16,64]{2,1,0:T(8,128)S(1)} %broadcast_multiply_fusion.2, f32[8,16]{1,0:T(8,128)S(1)} %get-tuple-element.28, f32[8,256]{1,0:T(8,128)S(1)} %get-tuple-element.23, ...), kind=kOutput, calls=%fused_computation.19 | convolution fusion | flops 37748736 | bytes 8512512 | tf_op jit(solution)/shard_map/rhpn,rn->rhp/dot_general | solution.py:106
  479.9 13.9 %psum.58 = f32[8,4]{0,1:T(4,128)S(1)} all-reduce(f32[8,4]{0,1:T(4,128)S(1)} %broadcast_multiply_fusion.6), channel_id=1, replica_groups=mesh['dp'=4,'tp'=8] {'tp'}, use_global_device_ids=true, to_apply=%region_11.12 | all-reduce | flops 32 | bytes 256 | tf_op jit(solution)/shard_map/psum | solution.py:111
  493.9 4.6 fusion.82
  498.6 27.7 %all-reduce.5 = bf16[8,4096]{1,0:T(8,128)(2,1)S(1)} all-reduce(f32[8,4096]{1,0:T(8,128)S(1)} %fusion.82), channel_id=1, replica_groups=mesh['dp'=4,'tp'=8] {'tp'}, use_global_device_ids=true, to_apply=%region_13.14 | all-reduce | flops 32768 | bytes 196608 | tf_op jit(solution)/shard_map/psum | solution.py:115
  526.5 10.2 %fusion.33 = f32[8,2,1024]{2,0,1:T(8,128)S(1)} fusion(bf16[2,1024,4096]{2,1,0:T(8,128)(2,1)} %bitcast.208, bf16[8,4096]{1,0:T(8,128)(2,1)S(1)} %multiply_convert_fusion.1), kind=kOutput, calls=%fused_computation.70 | convolution fusion | flops 134217728 | bytes 16908288 | tf_op jit(solution)/shard_map/dot_general | solution.py:87
  536.9 0.4 convolution_bitcast_fusion.1
  537.4 14.0 %all_gather.22 = f32[8,2048]{1,0:T(8,128)S(1)} all-gather(f32[8,256]{1,0:T(8,128)S(1)} %divide_multiply_fusion.5), channel_id=1, replica_groups=mesh['dp'=4,'tp'=8] {'tp'}, dimensions={1}, use_global_device_ids=true | all-gather | bytes 73728 | tf_op jit(solution)/shard_map/all_gather | solution.py:95
  551.6 14.5 %fusion.2 = f32[8,1,16,64]{3,1,2,0:T(1,128)S(1)} fusion(f32[8,256]{1,0:T(8,128)S(1)} %get-tuple-element.15, f32[8,16,64]{2,1,0:T(8,128)S(1)} %broadcast_multiply_fusion.1, f32[8,16]{1,0:T(8,128)S(1)} %get-tuple-element.30, f32[8,16,64,256]{3,2,1,0:T(8,128)} %param.33, f32[8,256]{1,0:T(8,128)S(1)} %get-tuple-element.19, ...), kind=kOutput, calls=%fused_computation.10 | convolution fusion | flops 44040192 | bytes 8553984 | tf_op jit(solution)/shard_map/rhpn,rn->rhp/dot_general | solution.py:106
  566.4 13.9 %psum.60 = f32[8,4]{0,1:T(4,128)S(1)} all-reduce(f32[8,4]{0,1:T(4,128)S(1)} %broadcast_multiply_fusion.5), channel_id=1, replica_groups=mesh['dp'=4,'tp'=8] {'tp'}, use_global_device_ids=true, to_apply=%region_18.19 | all-reduce | flops 32 | bytes 256 | tf_op jit(solution)/shard_map/psum | solution.py:111
  580.5 4.6 fusion.80
  585.1 27.2 %all-reduce.6 = bf16[8,4096]{1,0:T(8,128)(2,1)S(1)} all-reduce(f32[8,4096]{1,0:T(8,128)S(1)} %fusion.80), channel_id=1, replica_groups=mesh['dp'=4,'tp'=8] {'tp'}, use_global_device_ids=true, to_apply=%region_20.21 | all-reduce | flops 32768 | bytes 196608 | tf_op jit(solution)/shard_map/psum | solution.py:115
  612.6 10.2 %fusion.31 = f32[8,2,1024]{2,0,1:T(8,128)S(1)} fusion(bf16[2,1024,4096]{2,1,0:T(8,128)(2,1)} %bitcast.209, bf16[8,4096]{1,0:T(8,128)(2,1)S(1)} %multiply_convert_fusion), kind=kOutput, calls=%fused_computation.68 | convolution fusion | flops 134217728 | bytes 16908288 | tf_op jit(solution)/shard_map/dot_general | solution.py:87
  623.0 0.4 convolution_bitcast_fusion
  623.5 14.2 %all_gather.23 = f32[8,2048]{1,0:T(8,128)S(1)} all-gather(f32[8,256]{1,0:T(8,128)S(1)} %divide_multiply_fusion.4), channel_id=1, replica_groups=mesh['dp'=4,'tp'=8] {'tp'}, dimensions={1}, use_global_device_ids=true | all-gather | bytes 73728 | tf_op jit(solution)/shard_map/all_gather | solution.py:95
  637.8 7.7 %multiply_add_fusion = f32[8,16,64,256]{3,2,1,0:T(8,128)S(1)} fusion(f32[8,256]{1,0:T(8,128)S(1)} %get-tuple-element.11, f32[8,16,64]{2,1,0:T(8,128)S(1)} %broadcast_multiply_fusion, f32[8,16]{1,0:T(8,128)S(1)} %get-tuple-element.32, f32[8,256]{1,0:T(8,128)S(1)} %get-tuple-element.15, f32[8,16,64]{2,1,0:T(8,128)S(1)} %broadcast_multiply_fusion.1, ...), kind=kLoop, calls=%fused_computation.5 | loop fusion | flops 25165824 | bytes 16943104 | tf_op jit(solution)/shard_map/add | solution.py:102
  645.5 3.4 copy-done.1
  648.9 9.8 %fusion.99 = f32[8,1,16,64]{3,1,2,0:T(1,128)S(1)} fusion(f32[8,16,64,256]{3,2,1,0:T(8,128)S(1)} %multiply_add_fusion, f32[8,256,1,1]{1,0,2,3:T(8,128)S(1)} %get-tuple-element.10), kind=kOutput, calls=%fused_computation.172 | convolution fusion | flops 25165824 | bytes 8429568 | tf_op jit(solution)/shard_map/rhpn,rn->rhp/dot_general | solution.py:106
  659.1 13.9 %psum.62 = f32[8,4]{0,1:T(4,128)S(1)} all-reduce(f32[8,4]{0,1:T(4,128)S(1)} %broadcast_multiply_fusion.4), channel_id=1, replica_groups=mesh['dp'=4,'tp'=8] {'tp'}, use_global_device_ids=true, to_apply=%region_25.26 | all-reduce | flops 32 | bytes 256 | tf_op jit(solution)/shard_map/psum | solution.py:111
  673.2 4.6 fusion.78
  677.8 27.2 %all-reduce.7 = bf16[8,4096]{1,0:T(8,128)(2,1)S(1)} all-reduce(f32[8,4096]{1,0:T(8,128)S(1)} %fusion.78), channel_id=1, replica_groups=mesh['dp'=4,'tp'=8] {'tp'}, use_global_device_ids=true, to_apply=%region_27.28 | all-reduce | flops 32768 | bytes 196608 | tf_op jit(solution)/shard_map/psum | solution.py:115
  705.0 0.6 pad_maximum_fusion.6
  (117 shorter events, 4.9 us)
Async XLA Ops:
  7.2 156.0 %copy-start = (bf16[4096,256]{1,0:T(8,128)(2,1)S(1)}, bf16[4096,256]{1,0:T(8,128)(2,1)}, u32[]{:S(2)}) copy-start(bf16[4096,256]{1,0:T(8,128)(2,1)} %param.24) | copy-start | bytes 6291460
  7.2 170.9 %all-gather.5.cloned.1.call-start = ((), (), s32[]{:S(2)}) async-start(), calls=%async_computation.2 | async-start | bytes 10485760 | tf_op jit(solution)/shard_map/all_gather | solution.py:68
  12.6 21.5 %copy-start.10 = (s32[8,2,8]{2,1,0:T(2,128)S(1)}, s32[8,2,8]{2,1,0:T(2,128)}, u32[]{:S(2)}) copy-start(s32[8,2,8]{2,1,0:T(2,128)} %param.23) | copy-start | bytes 1540
  27.6 100.5 %all-to-all-start = ((bf16[128,2,8192]{0,1,2:T(2,128)(2,1)}), bf16[128,2,8192]{0,1,2:T(2,128)(2,1)}, u32[]{:S(2)}, u32[]{:S(2)}) async-start(bf16[128,2,8192]{0,1,2:T(2,128)(2,1)} %copy.29), calls=%async_computation | async-start | bytes 8388608 | tf_op jit(solution)/shard_map/all_to_all | solution.py:58
  34.0 285.2 %all-gather.3.cloned.1.call-start = ((), (), s32[]{:S(2)}) async-start(), calls=%async_computation.1 | async-start | bytes 20971520 | tf_op jit(solution)/shard_map/all_gather | solution.py:61
  153.6 9.1 %copy-start.13 = (f32[5,256]{1,0:T(8,128)S(1)}, f32[5,256]{1,0:T(8,128)}, u32[]{:S(2)}) copy-start(f32[5,256]{1,0:T(8,128)} %param.27) | copy-start | bytes 15364
  153.6 9.2 %copy-start.8 = (bf16[8,3,256]{2,0,1:T(8,128)(2,1)S(1)}, bf16[8,3,256]{2,0,1:T(8,128)(2,1)}, u32[]{:S(2)}) copy-start(bf16[8,3,256]{2,0,1:T(8,128)(2,1)} %param.32) | copy-start | bytes 36868
  153.6 9.2 %copy-start.7 = (f32[5,1024]{1,0:T(8,128)S(1)}, f32[5,1024]{1,0:T(8,128)}, u32[]{:S(2)}) copy-start(f32[5,1024]{1,0:T(8,128)} %param.26) | copy-start | bytes 61444
  153.6 9.2 %copy-start.6 = (bf16[8,3,1024]{2,0,1:T(8,128)(2,1)S(1)}, bf16[8,3,1024]{2,0,1:T(8,128)(2,1)}, u32[]{:S(2)}) copy-start(bf16[8,3,1024]{2,0,1:T(8,128)(2,1)} %param.31) | copy-start | bytes 147460
  153.6 9.3 %copy-start.2 = (bf16[4,8,4096]{2,1,0:T(8,128)(2,1)S(1)}, bf16[4,8,4096]{2,1,0:T(8,128)(2,1)}, u32[]{:S(2)}) copy-start(bf16[4,8,4096]{2,1,0:T(8,128)(2,1)} %param.19) | copy-start | bytes 786436
  153.6 9.5 %copy-start.5 = (f32[4096]{0:T(1024)S(1)}, f32[4096]{0:T(1024)}, u32[]{:S(2)}) copy-start(f32[4096]{0:T(1024)} %param.20) | copy-start | bytes 49156
  153.7 24.1 %copy-start.3 = (bf16[4096,16]{0,1:T(8,128)(2,1)S(1)}, bf16[4096,16]{0,1:T(8,128)(2,1)}, u32[]{:S(2)}) copy-start(bf16[4096,16]{0,1:T(8,128)(2,1)} %param.25) | copy-start | bytes 393220
  153.7 24.1 %copy-start.11 = (f32[16]{0:T(128)S(1)}, f32[16]{0:T(128)}, u32[]{:S(2)}) copy-start(f32[16]{0:T(128)} %param.29) | copy-start | bytes 196
  153.7 24.1 %copy-start.12 = (f32[16]{0:T(128)S(1)}, f32[16]{0:T(128)}, u32[]{:S(2)}) copy-start(f32[16]{0:T(128)} %param.28) | copy-start | bytes 196
  378.5 13.4 %copy-start.9 = (f32[16]{0:T(128)S(1)}, f32[16]{0:T(128)}, u32[]{:S(2)}) copy-start(f32[16]{0:T(128)} %param.30) | copy-start | bytes 196
  378.5 30.2 %copy-start.4 = (f32[1024]{0:T(1024)S(1)}, f32[1024]{0:T(1024)}, u32[]{:S(2)}) copy-start(f32[1024]{0:T(1024)} %param.34) | copy-start | bytes 12292
  645.5 3.4 copy-start.1
Sparse Core Ops, SparseCore 0:
  12.7 90.1 all-gather.4
  162.9 156.2 all-gather.2
where the time goes:
time: 721 us; the launch traced here: 713 us
  blocking collectives  224 us (31%)
  waiting for transfers between devices  210 us (29%)
  matrix products  113 us (16%)
  local copies, waits for them, and re-layouts  81.8 us (11%)
  other arithmetic  63.1 us (9%)
  between operations  14.8 us (2%)
    all_gather x1, waiting for transfers between devices, body(): lax.all_gather(zx_delta.astype(jnp.bfloat16), 'dp', axis=0, tiled=True)  131 us
    psum x4, blocking collectives, body(): whole = lax.psum(partial_value, 'tp').astype(jnp.bfloat16)  109 us
    all_to_all x1, waiting for transfers between devices, body(): lax.all_to_all(zx_codes, 'tp', split_axis=2, concat_axis=0, tiled=True)  79.2 us
    psum x4, blocking collectives, body(): totals = lax.psum(squares[:, None] * group_mask, 'tp')  58.1 us
    all_gather x4, blocking collectives, body(): bc_all = lax.all_gather(conv_piece, 'tp', axis=1, tiled=True)  56.3 us
    dot_general x4, matrix products, body(): jnp.einsum('rhpn,rn->rhp', state, c_group, precision=lax.Precision.HIGHEST)  51.1 us
    dot_general x4, matrix products, body(): zx = jnp.dot(normed, zx_weights, preferred_element_type=jnp.float32)  40.7 us
    unnamed x30, local copies, waits for them, and re-layouts  27.7 us
  transfers between devices with their start and end apart: 3, of which 2 were waited for; matrix products, arithmetic and copies ran while one was open for 11% of the time, Pallas kernels for 0%

commit v1 on v0

--- a/solution.py
+++ b/solution.py
@@ -92,7 +92,17 @@
         dt_raw = jnp.dot(normed, w_dt, preferred_element_type=jnp.float32)
         conv_inner, history_x = conv_step(history_x, inner, conv_x)
         conv_piece, history_bc = conv_step(history_bc, bc_raw, conv_bc)
-        bc_all = lax.all_gather(conv_piece, "tp", axis=1, tiled=True)
+        lanes = lax.psum(1, "tp")
+        view_out = sorted(((rr, (rr + 1) % lanes) for rr in range(lanes)))
+        z1 = conv_piece
+        pages = [z1]
+        for h in [*range(1, lanes)]:
+            z1 = lax.ppermute(z1, "tp", view_out)
+            pages.insert(0, z1)
+        piece_next = jnp.concatenate(pages, axis=1)
+        e_next = lax.axis_index("tp")
+        v_next = e_next + 1
+        bc_all = jnp.roll(piece_next, shift=v_next * conv_piece.shape[1], axis=1)
         b_group = lax.dynamic_slice_in_dim(bc_all, group * states_n, states_n, 1)
         c_group = lax.dynamic_slice_in_dim(bc_all, G * states_n + group * states_n, states_n, 1)
         step_size = jax.nn.softplus(dt_raw + dt_bias)

time: 721 us -> 770 us (1.068)
  waiting for transfers between devices: 210 us -> 315 us
  blocking collectives: 224 us -> 166 us
    ppermute x0 -> x28, waiting for transfers between devices: none -> 125 us  [body(): z1 = lax.ppermute(z1, 'tp', view_out)]
    all_gather x4 -> x0, blocking collectives: 56.3 us -> none  [body(): bc_all = lax.all_gather(conv_piece, 'tp', axis=1, tiled=True)]
    all_gather x1, waiting for transfers between devices: 131 us -> 111 us  [body(): lax.all_gather(zx_delta.astype(jnp.bfloat16), 'dp', axis=0, tiled=True)]
    unnamed x30 -> x58, local copies, waits for them, and re-layouts: 27.7 us -> 27.8 us
  transfers between devices with their start and end apart: 3 -> 31, of which waited for: 2 -> 28; matrix products, arithmetic and copies ran while one was open for 11% -> 13% of each run, Pallas kernels for 0% -> 0%
where the time goes in v1:
time: 770 us; the launch traced here: 761 us
  waiting for transfers between devices  315 us (41%)
  blocking collectives  166 us (22%)
  matrix products  113 us (15%)
  local copies, waits for them, and re-layouts  81.8 us (11%)
  other arithmetic  63.6 us (8%)
  between operations  15 us (2%)
    ppermute x28, waiting for transfers between devices, body(): z1 = lax.ppermute(z1, 'tp', view_out)  125 us
    all_gather x1, waiting for transfers between devices, body(): lax.all_gather(zx_delta.astype(jnp.bfloat16), 'dp', axis=0, tiled=True)  111 us
    psum x4, blocking collectives, body(): whole = lax.psum(partial_value, 'tp').astype(jnp.bfloat16)  109 us
    all_to_all x1, waiting for transfers between devices, body(): lax.all_to_all(zx_codes, 'tp', split_axis=2, concat_axis=0, tiled=True)  79.2 us
    psum x4, blocking collectives, body(): totals = lax.psum(squares[:, None] * group_mask, 'tp')  56.9 us
    dot_general x4, matrix products, body(): jnp.einsum('rhpn,rn->rhp', state, c_group, precision=lax.Precision.HIGHEST)  51.1 us
    dot_general x4, matrix products, body(): zx = jnp.dot(normed, zx_weights, preferred_element_type=jnp.float32)  40.7 us
    unnamed x58, local copies, waits for them, and re-layouts  27.8 us
  transfers between devices with their start and end apart: 31, of which 28 were waited for; matrix products, arithmetic and copies ran while one was open for 13% of the time, Pallas kernels for 0%

profile of v1, /device:TPU:0, one launch (start us, length us, event | category | flops | bytes accessed | tf_op | source)
XLA Modules:
  0.0 761.5 jit_solution(18243680015152721995)
XLA Ops:
  12.6 15.0 %copy.29 = bf16[128,2,8192]{0,1,2:T(2,128)(2,1)} copy(bf16[128,2,8192]{2,1,0:T(2,128)(2,1)} %param.24) | data formatting | bytes 8388608 | tf_op args[3]
  27.6 6.4 all-to-all-start
  38.1 10.8 %mul.616 = f32[1024,2,1024]{2,1,0:T(2,128)} reshape(f32[8,128,2,8,128]{4,3,2,1,0:T(8,128)} %mul.615) | data formatting | bytes 16777216 | tf_op jit(solution)/shard_map/mul | solution.py:19
  48.8 79.2 %all-to-all-done = bf16[128,2,8192]{0,1,2:T(2,128)(2,1)} async-done(((bf16[128,2,8192]{0,1,2:T(2,128)(2,1)}), bf16[128,2,8192]{0,1,2:T(2,128)(2,1)}, u32[]{:S(2)}, u32[]{:S(2)}) %all-to-all-start) | async-done | bytes 4194336 | tf_op jit(solution)/shard_map/all_to_all | solution.py:58
  128.1 8.5 %convert_bitcast_fusion = f32[8,128,2,1024]{1,2,3,0:T(2,128)} fusion(bf16[128,2,8,1024]{0,1,3,2:T(2,128)(2,1)} %bitcast.39), kind=kLoop, calls=%fused_computation.2 | loop fusion | flops 2097152 | bytes 12582912 | tf_op jit(solution)/shard_map/convert_element_type | solution.py:17
  136.5 17.1 %copy.30 = f32[8,128,2,1024]{3,2,1,0:T(2,128)} copy(f32[8,128,2,1024]{1,2,3,0:T(2,128)} %convert_bitcast_fusion) | data formatting | bytes 16777216 | tf_op jit(solution)/shard_map/convert_element_type | solution.py:17
  153.7 9.1 %fusion = bf16[1024,2,1024]{2,1,0:T(2,128)(2,1)} fusion(f32[1024,2,1024]{2,1,0:T(2,128)} %mul.616, f32[8,128,2,1024]{3,2,1,0:T(2,128)} %copy.30), kind=kLoop, calls=%fused_computation.4 | loop fusion | flops 4194304 | bytes 20971520 | tf_op jit(solution)/shard_map/convert_element_type | solution.py:61
  163.6 4.9 collective-permute-done
  168.4 4.9 collective-permute-done.1
  173.3 4.9 collective-permute-done.2
  183.1 4.8 collective-permute-done.4
  187.9 4.9 collective-permute-done.5
  198.0 10.1 %add_convert_fusion.1 = bf16[1024,4096]{1,0:T(8,128)(2,1)} fusion(bf16[1024,4096]{1,0:T(8,128)(2,1)} %all-gather.5.cloned.1.call-done, bf16[1024,4096]{1,0:T(8,128)(2,1)} %param.37), kind=kLoop, calls=%fused_computation.1 | loop fusion | flops 16777216 | bytes 25165824 | tf_op jit(solution)/shard_map/convert_element_type | solution.py:69
  208.1 111.1 %all-gather.3.cloned.1.call-done = bf16[4096,2,1024]{2,1,0:T(2,128)(2,1)} async-done(((bf16[1024,2,1024]{2,1,0:T(2,128)(2,1)}), bf16[4096,2,1024]{2,1,0:T(2,128)(2,1)}) %all-gather.3.cloned.1.call-update) | async-done | bytes 16777232 | tf_op jit(solution)/shard_map/all_gather | solution.py:61
  319.2 19.2 %add_convert_fusion = bf16[4096,2,1024]{2,1,0:T(2,128)(2,1)S(1)} fusion(bf16[4096,2,1024]{2,1,0:T(2,128)(2,1)} %all-gather.3.cloned.1.call-done, bf16[4096,2,1024]{2,1,0:T(2,128)(2,1)} %param.23), kind=kLoop, calls=%fused_computation | loop fusion | flops 33554432 | bytes 50331648 | tf_op jit(solution)/shard_map/convert_element_type | solution.py:64
  338.4 9.3 %copy.40 = bf16[512,8,2,1024]{3,1,2,0:T(8,128)(2,1)} copy(bf16[512,8,2,1024]{3,2,1,0:T(2,128)(2,1)S(1)} %bitcast.210) | data formatting | bytes 33554432
  347.7 20.7 %copy.31 = bf16[2048,4096]{1,0:T(8,128)(2,1)} copy(bf16[2048,4096]{0,1:T(8,128)(2,1)} %bitcast.211) | data formatting | bytes 33554432 | tf_op jit(solution)/shard_map/dot_general | solution.py:87
  368.4 10.2 %fusion.29 = f32[8,2,1024]{2,0,1:T(8,128)S(1)} fusion(bf16[2,1024,4096]{2,1,0:T(8,128)(2,1)} %bitcast.206, f32[4096]{0:T(1024)S(1)} %copy-done.5, f32[8]{0:T(128)S(1)} %add_rsqrt_fusion.7, bf16[4,8,4096]{2,1,0:T(8,128)(2,1)S(1)} %copy-done.2), kind=kOutput, calls=%fused_computation.115 | convolution fusion | flops 134348800 | bytes 16925184 | tf_op jit(solution)/shard_map/dot_general | solution.py:87
  378.9 13.1 %fusion.1 = f32[8,1,16,64]{3,1,2,0:T(1,128)S(1)} fusion(f32[8,16,64,256]{3,2,1,0:T(8,128)} %param.35, f32[8,256]{1,0:T(8,128)S(1)} %get-tuple-element.24, f32[8,16,64]{2,1,0:T(8,128)S(1)} %broadcast_multiply_fusion.3, f32[8,16]{1,0:T(8,128)S(1)} %get-tuple-element.27, f32[8,256,1,1]{1,0,2,3:T(8,128)S(1)} %get-tuple-element.23), kind=kOutput, calls=%fused_computation.9 | convolution fusion | flops 31457280 | bytes 8471040 | tf_op jit(solution)/shard_map/rhpn,rn->rhp/dot_general | solution.py:116
  392.2 16.2 %psum.56 = f32[8,4]{0,1:T(4,128)S(1)} all-reduce(f32[8,4]{0,1:T(4,128)S(1)} %broadcast_multiply_fusion.7), channel_id=1, replica_groups=mesh['dp'=4,'tp'=8] {'tp'}, use_global_device_ids=true, to_apply=%region_4.6 | all-reduce | flops 32 | bytes 256 | tf_op jit(solution)/shard_map/psum | solution.py:121
  413.2 27.4 %all-reduce.4 = bf16[8,4096]{1,0:T(8,128)(2,1)S(1)} all-reduce(f32[8,4096]{1,0:T(8,128)S(1)} %fusion.84), channel_id=1, replica_groups=mesh['dp'=4,'tp'=8] {'tp'}, use_global_device_ids=true, to_apply=%region_6.8 | all-reduce | flops 32768 | bytes 196608 | tf_op jit(solution)/shard_map/psum | solution.py:125
  440.8 10.2 %fusion.35 = f32[8,2,1024]{2,0,1:T(8,128)S(1)} fusion(bf16[2,1024,4096]{2,1,0:T(8,128)(2,1)} %bitcast.207, bf16[8,4096]{1,0:T(8,128)(2,1)S(1)} %multiply_convert_fusion.2), kind=kOutput, calls=%fused_computation.120 | convolution fusion | flops 134217728 | bytes 16908288 | tf_op jit(solution)/shard_map/dot_general | solution.py:87
  451.7 4.8 collective-permute-done.7
  456.6 4.9 collective-permute-done.8
  466.4 4.8 collective-permute-done.10
  471.2 4.9 collective-permute-done.11
  476.1 4.9 collective-permute-done.12
  481.0 4.8 collective-permute-done.13
  486.0 13.7 %fusion.10 = f32[8,1,16,64]{3,1,2,0:T(1,128)S(1)} fusion(f32[8,16,64,256]{3,2,1,0:T(8,128)} %param.35, f32[8,256]{1,0:T(8,128)S(1)} %get-tuple-element.20, f32[8,16,64]{2,1,0:T(8,128)S(1)} %broadcast_multiply_fusion.2, f32[8,16]{1,0:T(8,128)S(1)} %get-tuple-element.29, f32[8,256]{1,0:T(8,128)S(1)} %get-tuple-element.24, ...), kind=kOutput, calls=%fused_computation.19 | convolution fusion | flops 37748736 | bytes 8512512 | tf_op jit(solution)/shard_map/rhpn,rn->rhp/dot_general | solution.py:116
  500.0 13.6 %psum.58 = f32[8,4]{0,1:T(4,128)S(1)} all-reduce(f32[8,4]{0,1:T(4,128)S(1)} %broadcast_multiply_fusion.6), channel_id=1, replica_groups=mesh['dp'=4,'tp'=8] {'tp'}, use_global_device_ids=true, to_apply=%region_11.13 | all-reduce | flops 32 | bytes 256 | tf_op jit(solution)/shard_map/psum | solution.py:121
  518.3 27.1 %all-reduce.5 = bf16[8,4096]{1,0:T(8,128)(2,1)S(1)} all-reduce(f32[8,4096]{1,0:T(8,128)S(1)} %fusion.82), channel_id=1, replica_groups=mesh['dp'=4,'tp'=8] {'tp'}, use_global_device_ids=true, to_apply=%region_13.15 | all-reduce | flops 32768 | bytes 196608 | tf_op jit(solution)/shard_map/psum | solution.py:125
  546.6 10.2 %fusion.33 = f32[8,2,1024]{2,0,1:T(8,128)S(1)} fusion(bf16[2,1024,4096]{2,1,0:T(8,128)(2,1)} %bitcast.208, bf16[8,4096]{1,0:T(8,128)(2,1)S(1)} %multiply_convert_fusion.1), kind=kOutput, calls=%fused_computation.118 | convolution fusion | flops 134217728 | bytes 16908288 | tf_op jit(solution)/shard_map/dot_general | solution.py:87
  561.7 4.9 collective-permute-done.16
  571.6 4.8 collective-permute-done.18
  576.4 4.9 collective-permute-done.19
  581.3 4.8 collective-permute-done.20
  586.2 14.5 %fusion.2 = f32[8,1,16,64]{3,1,2,0:T(1,128)S(1)} fusion(f32[8,256]{1,0:T(8,128)S(1)} %get-tuple-element.16, f32[8,16,64]{2,1,0:T(8,128)S(1)} %broadcast_multiply_fusion.1, f32[8,16]{1,0:T(8,128)S(1)} %get-tuple-element.31, f32[8,16,64,256]{3,2,1,0:T(8,128)} %param.35, f32[8,256]{1,0:T(8,128)S(1)} %get-tuple-element.20, ...), kind=kOutput, calls=%fused_computation.10 | convolution fusion | flops 44040192 | bytes 8553984 | tf_op jit(solution)/shard_map/rhpn,rn->rhp/dot_general | solution.py:116
  601.0 13.6 %psum.60 = f32[8,4]{0,1:T(4,128)S(1)} all-reduce(f32[8,4]{0,1:T(4,128)S(1)} %broadcast_multiply_fusion.5), channel_id=1, replica_groups=mesh['dp'=4,'tp'=8] {'tp'}, use_global_device_ids=true, to_apply=%region_18.20 | all-reduce | flops 32 | bytes 256 | tf_op jit(solution)/shard_map/psum | solution.py:121
  619.4 27.1 %all-reduce.6 = bf16[8,4096]{1,0:T(8,128)(2,1)S(1)} all-reduce(f32[8,4096]{1,0:T(8,128)S(1)} %fusion.80), channel_id=1, replica_groups=mesh['dp'=4,'tp'=8] {'tp'}, use_global_device_ids=true, to_apply=%region_20.22 | all-reduce | flops 32768 | bytes 196608 | tf_op jit(solution)/shard_map/psum | solution.py:125
  647.3 4.8 collective-permute-done.21
  652.2 10.2 %fusion.31 = f32[8,2,1024]{2,0,1:T(8,128)S(1)} fusion(bf16[2,1024,4096]{2,1,0:T(8,128)(2,1)} %bitcast.209, bf16[8,4096]{1,0:T(8,128)(2,1)S(1)} %multiply_convert_fusion), kind=kOutput, calls=%fused_computation.116 | convolution fusion | flops 134217728 | bytes 16908288 | tf_op jit(solution)/shard_map/dot_general | solution.py:87
  667.3 4.9 collective-permute-done.24
  672.2 4.8 collective-permute-done.25
  677.1 4.8 collective-permute-done.26
  687.1 7.7 %multiply_add_fusion = f32[8,16,64,256]{3,2,1,0:T(8,128)S(1)} fusion(f32[8,256]{1,0:T(8,128)S(1)} %get-tuple-element.12, f32[8,16,64]{2,1,0:T(8,128)S(1)} %broadcast_multiply_fusion, f32[8,16]{1,0:T(8,128)S(1)} %get-tuple-element.33, f32[8,256]{1,0:T(8,128)S(1)} %get-tuple-element.16, f32[8,16,64]{2,1,0:T(8,128)S(1)} %broadcast_multiply_fusion.1, ...), kind=kLoop, calls=%fused_computation.5 | loop fusion | flops 25165824 | bytes 16943104 | tf_op jit(solution)/shard_map/add | solution.py:112
  698.2 9.8 %fusion.107 = f32[8,1,16,64]{3,1,2,0:T(1,128)S(1)} fusion(f32[8,16,64,256]{3,2,1,0:T(8,128)S(1)} %multiply_add_fusion, f32[8,256,1,1]{1,0,2,3:T(8,128)S(1)} %get-tuple-element.11), kind=kOutput, calls=%fused_computation.228 | convolution fusion | flops 25165824 | bytes 8429568 | tf_op jit(solution)/shard_map/rhpn,rn->rhp/dot_general | solution.py:116
  708.3 13.6 %psum.62 = f32[8,4]{0,1:T(4,128)S(1)} all-reduce(f32[8,4]{0,1:T(4,128)S(1)} %broadcast_multiply_fusion.4), channel_id=1, replica_groups=mesh['dp'=4,'tp'=8] {'tp'}, use_global_device_ids=true, to_apply=%region_25.27 | all-reduce | flops 32 | bytes 256 | tf_op jit(solution)/shard_map/psum | solution.py:121
  726.7 27.1 %all-reduce.7 = bf16[8,4096]{1,0:T(8,128)(2,1)S(1)} all-reduce(f32[8,4096]{1,0:T(8,128)S(1)} %fusion.78), channel_id=1, replica_groups=mesh['dp'=4,'tp'=8] {'tp'}, use_global_device_ids=true, to_apply=%region_27.29 | all-reduce | flops 32768 | bytes 196608 | tf_op jit(solution)/shard_map/psum | solution.py:125
  (201 shorter events, 73.0 us)
Async XLA Ops:
  7.2 155.9 %copy-start = (bf16[4096,256]{1,0:T(8,128)(2,1)S(1)}, bf16[4096,256]{1,0:T(8,128)(2,1)}, u32[]{:S(2)}) copy-start(bf16[4096,256]{1,0:T(8,128)(2,1)} %param.26) | copy-start | bytes 6291460
  7.2 190.8 %all-gather.5.cloned.1.call-start = ((), (), s32[]{:S(2)}) async-start(), calls=%async_computation.2 | async-start | bytes 10485760 | tf_op jit(solution)/shard_map/all_gather | solution.py:68
  12.6 21.5 %copy-start.10 = (s32[8,2,8]{2,1,0:T(2,128)S(1)}, s32[8,2,8]{2,1,0:T(2,128)}, u32[]{:S(2)}) copy-start(s32[8,2,8]{2,1,0:T(2,128)} %param.25) | copy-start | bytes 1540
  27.6 100.5 %all-to-all-start = ((bf16[128,2,8192]{0,1,2:T(2,128)(2,1)}), bf16[128,2,8192]{0,1,2:T(2,128)(2,1)}, u32[]{:S(2)}, u32[]{:S(2)}) async-start(bf16[128,2,8192]{0,1,2:T(2,128)(2,1)} %copy.29), calls=%async_computation | async-start | bytes 8388608 | tf_op jit(solution)/shard_map/all_to_all | solution.py:58
  34.0 285.2 %all-gather.3.cloned.1.call-start = ((), (), s32[]{:S(2)}) async-start(), calls=%async_computation.1 | async-start | bytes 20971520 | tf_op jit(solution)/shard_map/all_gather | solution.py:61
  153.6 9.2 %copy-start.13 = (f32[5,256]{1,0:T(8,128)S(1)}, f32[5,256]{1,0:T(8,128)}, u32[]{:S(2)}) copy-start(f32[5,256]{1,0:T(8,128)} %param.29) | copy-start | bytes 15364
  153.6 9.2 %copy-start.8 = (bf16[8,3,256]{2,0,1:T(8,128)(2,1)S(1)}, bf16[8,3,256]{2,0,1:T(8,128)(2,1)}, u32[]{:S(2)}) copy-start(bf16[8,3,256]{2,0,1:T(8,128)(2,1)} %param.34) | copy-start | bytes 36868
  153.6 9.2 %copy-start.2 = (bf16[4,8,4096]{2,1,0:T(8,128)(2,1)S(1)}, bf16[4,8,4096]{2,1,0:T(8,128)(2,1)}, u32[]{:S(2)}) copy-start(bf16[4,8,4096]{2,1,0:T(8,128)(2,1)} %param.21) | copy-start | bytes 786436
  153.6 9.4 %copy-start.5 = (f32[4096]{0:T(1024)S(1)}, f32[4096]{0:T(1024)}, u32[]{:S(2)}) copy-start(f32[4096]{0:T(1024)} %param.22) | copy-start | bytes 49156
  153.6 24.5 %copy-start.3 = (bf16[4096,16]{0,1:T(8,128)(2,1)S(1)}, bf16[4096,16]{0,1:T(8,128)(2,1)}, u32[]{:S(2)}) copy-start(bf16[4096,16]{0,1:T(8,128)(2,1)} %param.27) | copy-start | bytes 393220
  153.6 24.5 %copy-start.11 = (f32[16]{0:T(128)S(1)}, f32[16]{0:T(128)}, u32[]{:S(2)}) copy-start(f32[16]{0:T(128)} %param.31) | copy-start | bytes 196
  153.7 24.5 %copy-start.12 = (f32[16]{0:T(128)S(1)}, f32[16]{0:T(128)}, u32[]{:S(2)}) copy-start(f32[16]{0:T(128)} %param.30) | copy-start | bytes 196
  153.7 29.4 %copy-start.7 = (f32[5,1024]{1,0:T(8,128)S(1)}, f32[5,1024]{1,0:T(8,128)}, u32[]{:S(2)}) copy-start(f32[5,1024]{1,0:T(8,128)} %param.28) | copy-start | bytes 61444
  153.7 39.3 %copy-start.6 = (bf16[8,3,1024]{2,0,1:T(8,128)(2,1)S(1)}, bf16[8,3,1024]{2,0,1:T(8,128)(2,1)}, u32[]{:S(2)}) copy-start(bf16[8,3,1024]{2,0,1:T(8,128)(2,1)} %param.33) | copy-start | bytes 147460
  163.5 4.9 collective-permute-start
  168.4 4.9 collective-permute-start.1
  173.3 4.9 collective-permute-start.2
  178.2 4.9 collective-permute-start.3
  183.0 4.9 collective-permute-start.4
  187.9 4.9 collective-permute-start.5
  192.8 5.0 collective-permute-start.6
  378.6 13.4 %copy-start.9 = (f32[16]{0:T(128)S(1)}, f32[16]{0:T(128)}, u32[]{:S(2)}) copy-start(f32[16]{0:T(128)} %param.32) | copy-start | bytes 196
  378.6 30.0 %copy-start.4 = (f32[1024]{0:T(1024)S(1)}, f32[1024]{0:T(1024)}, u32[]{:S(2)}) copy-start(f32[1024]{0:T(1024)} %param.36) | copy-start | bytes 12292
  451.6 4.9 collective-permute-start.7
  456.6 4.9 collective-permute-start.8
  461.4 4.9 collective-permute-start.9
  466.3 4.9 collective-permute-start.10
  471.2 4.9 collective-permute-start.11
  476.1 4.9 collective-permute-start.12
  480.9 4.9 collective-permute-start.13
  546.2 10.7 %collective-permute-start.14 = (f32[8,256]{1,0:T(8,128)S(1)}, f32[8,256]{1,0:T(8,128)S(1)}, u32[]{:S(2)}, u32[]{:S(2)}) collective-permute-start(f32[8,256]{1,0:T(8,128)S(1)} %divide_multiply_fusion.5), channel_id=1, source_target_pairs={{0,1},{1,2},{2,3},{3,4},{4,5},{5,6},{6,7},{7,0},{8,9},{9,10},{10,1... | collective-permute-start | bytes 24584 | tf_op jit(solution)/shard_map/ppermute | solution.py:100
  556.8 4.9 collective-permute-start.15
  561.7 4.9 collective-permute-start.16
  566.6 4.9 collective-permute-start.17
  571.5 4.9 collective-permute-start.18
  576.3 4.9 collective-permute-start.19
  581.2 4.9 collective-permute-start.20
  647.2 4.9 collective-permute-start.21
  652.2 10.2 %collective-permute-start.22 = (f32[8,256]{1,0:T(8,128)S(1)}, f32[8,256]{1,0:T(8,128)S(1)}, u32[]{:S(2)}, u32[]{:S(2)}) collective-permute-start(f32[8,256]{1,0:T(8,128)S(1)} %collective-permute-done.21), channel_id=1, source_target_pairs={{0,1},{1,2},{2,3},{3,4},{4,5},{5,6},{6,7},{7,0},{8,9},{9,10},{10,1... | collective-permute-start | bytes 24584 | tf_op jit(solution)/shard_map/ppermute | solution.py:100
  662.4 4.9 collective-permute-start.23
  667.3 4.9 collective-permute-start.24
  672.1 4.9 collective-permute-start.25
  677.0 4.9 collective-permute-start.26
  681.9 5.0 collective-permute-start.27
  694.8 3.4 copy-start.1
Sparse Core Ops, SparseCore 0:
  12.7 90.1 all-gather.4
  162.9 156.2 all-gather.2
